TPU v7x, 32 devices: a whole 2x2x4 slice. The times are simulated.
32 devices in a mesh: parts: 2 (over y), row: 4 (over x, core), col: 4 (over z).
Axes of the slice: x: 2, y: 2, z: 4, core: 2. Of those that a mesh axis runs over, the one named last changes fastest.
Arguments:
- left_factor: bfloat16 [6144, 8, 1024], P(('parts', 'col'), None, 'row'), parts along dimension 0, may hold values from -0.109375 to 0.109375
- right_factor: bfloat16 [64, 1024, 3072], P('parts', 'col', 'row'), parts along dimension 0, may hold values from -6 to 6
- amplitudes: bfloat16 [1024, 1024, 512], P('row', 'col', 'parts'), parts along dimension 2, may hold values from -0.0078125 to 0.0078125
Outputs:
- ladder: float32 [512, 256], P(('parts', 'row', 'col')), parts along dimension 0
There are 2 independent parts, one for each index of `parts`. A program takes and returns all parts, laid end to end along the dimension named above; each array names one. Nothing has to cross between parts.
All inputs are finite; a program needn't handle non-finite values.
Results may differ from a plain program's by a relative error of at most 0.0029.
Values may be sent and summed in bfloat16 or wider, within the bound.
A program may use at most 192 MiB of HBM per device.

v0:
```python
import jax
import jax.numpy as jnp
from jax import lax
from jax.sharding import PartitionSpec as P


def contract_aux(left_rows, right_rows):
    return lax.dot_general(
        left_rows, right_rows, (((0,), (1,)), ((), ())), preferred_element_type=jnp.float32
    )


def on_device(left_factor, right_factor, amplitudes):
    width_a = left_factor.shape[1]
    span_c = left_factor.shape[2]
    width_b = right_factor.shape[0]
    span_d = right_factor.shape[1]
    pair_count = amplitudes.shape[2]
    left_all = lax.all_gather(left_factor, "col", axis=0, tiled=True)
    left_flat = left_all.reshape(left_all.shape[0], width_a * span_c)
    shard_part = lax.all_gather(right_factor, "row", axis=2, tiled=True)
    length = shard_part.shape[2]
    integral = contract_aux(left_flat, shard_part.reshape(width_b * span_d, length))
    rounded = integral.astype(jnp.bfloat16).reshape(width_a, span_c, width_b, span_d)
    partial_sums = jnp.einsum(
        "cdp,acbd->pab", amplitudes, rounded, preferred_element_type=jnp.float32
    ).reshape(pair_count, width_a * width_b)
    return lax.psum_scatter(partial_sums, ("row", "col"), scatter_dimension=0, tiled=True)


def solution(mesh):
    return jax.shard_map(
        on_device,
        mesh=mesh,
        in_specs=(
            P(("parts", "col"), None, "row"),
            P("parts", "col", "row"),
            P("row", "col", "parts"),
        ),
        out_specs=P(("parts", "row", "col"), None),
        check_vma=False,
    )
```

profile of v0, /device:TPU:0, one launch (start us, length us, event | category | flops | bytes accessed | tf_op | source)
XLA Modules:
  0.0 753.3 jit_solution(4722424935364290025)
XLA Ops:
  6.5 0.0 all-gather.3.cloned.1.call-start
  6.5 0.7 all-gather.3.cloned.1.call-update
  7.3 0.0 all-gather.5.cloned.1.call-start
  7.3 0.7 all-gather.5.cloned.1.call-update
  8.0 0.0 reduce-scatter.2.cloned.1.call-start
  8.1 221.8 %all-gather.3.cloned.1.call-done = bf16[3072,8,256]{2,1,0:T(8,128)(2,1)} async-done(((bf16[768,8,256]{2,1,0:T(8,128)(2,1)}), bf16[3072,8,256]{2,1,0:T(8,128)(2,1)}) %all-gather.3.cloned.1.call-update) | async-done | bytes 12582928 | tf_op jit(solution)/shard_map/all_gather | solution.py:19
  229.8 13.5 %copy.7 = bf16[384,8,8,256]{3,1,2,0:T(8,128)(2,1)} copy(bf16[384,8,8,256]{3,2,1,0:T(8,128)(2,1)} %bitcast.23) | data formatting | bytes 25165824
  243.3 285.9 %all-gather.5.cloned.1.call-done = bf16[32,256,3072]{2,1,0:T(8,128)(2,1)} async-done(((bf16[32,256,768]{2,1,0:T(8,128)(2,1)}), bf16[32,256,3072]{2,1,0:T(8,128)(2,1)}) %all-gather.5.cloned.1.call-update) | async-done | bytes 50331664 | tf_op jit(solution)/shard_map/all_gather | solution.py:21
  529.2 115.1 %convolution_convert_fusion = bf16[2048,8192]{1,0:T(8,128)(2,1)} fusion(bf16[3072,2048]{1,0:T(8,128)(2,1)} %bitcast.24, bf16[8192,3072]{1,0:T(8,128)(2,1)} %bitcast.26), kind=kOutput, calls=%fused_computation.3 | convolution fusion | flops 103095992320 | bytes 96468992 | tf_op jit(solution)/shard_map/dot_general | solution.py:8
  644.3 23.0 %copy.8 = bf16[256,8,32,256]{3,2,1,0:T(8,128)(2,1)} copy(bf16[256,8,32,256]{3,1,2,0:T(8,128)(2,1)} %bitcast.22) | data formatting | bytes 67108864
  667.3 22.7 %fusion = f32[8,32,256,1]{2,1,3,0:T(8,128)S(1)} fusion(bf16[256,256,256]{2,1,0:T(8,128)(2,1)} %param.5, bf16[8,256,32,256]{3,2,1,0:T(8,128)(2,1)} %bitcast.21), kind=kOutput, calls=%fused_computation | convolution fusion | flops 8589934592 | bytes 67371008 | tf_op jit(solution)/shard_map/cdp,acbd->pab/dot_general | solution.py:25
  690.0 0.8 copy.5
  690.9 0.0 reduce-scatter.2.cloned.1.call-update
  690.9 55.9 %reduce-scatter.2.cloned.1.call-done = f32[16,256]{1,0:T(8,128)} async-done(((f32[256,256]{1,0:T(8,128)}), f32[16,256]{1,0:T(8,128)}) %reduce-scatter.2.cloned.1.call-update) | async-done | bytes 16400 | tf_op jit(solution)/shard_map/reduce_scatter | solution.py:28
Async XLA Ops:
  6.5 223.3 %all-gather.3.cloned.1.call-start = ((), (), s32[]{:S(2)}) async-start(), calls=%async_computation.1 | async-start | bytes 15728640 | tf_op jit(solution)/shard_map/all_gather | solution.py:19
  7.3 521.9 %all-gather.5.cloned.1.call-start = ((), (), s32[]{:S(2)}) async-start(), calls=%async_computation.2 | async-start | bytes 62914560 | tf_op jit(solution)/shard_map/all_gather | solution.py:21
  8.0 738.8 %reduce-scatter.2.cloned.1.call-start = ((), (), s32[]{:S(2)}) async-start(), calls=%async_computation.3 | async-start | bytes 278528 | tf_op jit(solution)/shard_map/reduce_scatter | solution.py:28
Sparse Core Ops, SparseCore 0:
  8.9 220.8 all-gather.2
  231.4 297.7 all-gather.4
  691.0 55.7 reduce-scatter.1
where the time goes:
time: 754 us; the launch traced here: 753 us
  waiting for transfers between devices  565 us (75%)
  matrix products  138 us (18%)
  local copies, waits for them, and re-layouts  37.4 us (5%)
  between operations  13.1 us (2%)
    all_gather x1, waiting for transfers between devices, on_device(): shard_part = lax.all_gather(right_factor, 'row', axis=2, tiled=True)  286 us
    all_gather x1, waiting for transfers between devices, on_device(): left_all = lax.all_gather(left_factor, 'col', axis=0, tiled=True)  222 us
    dot_general x1, matrix products, contract_aux(): lax.dot_general(left_rows, right_rows, (((0,), (1,)), ((), ())), preferre...  115 us
    reduce_scatter x1, waiting for transfers between devices, on_device(): lax.psum_scatter(partial_sums, ('row', 'col'), scatter_dimension=0, tiled...  55.9 us
    unnamed x2, local copies, waits for them, and re-layouts  36.5 us
    dot_general x1, matrix products, on_device(): jnp.einsum('cdp,acbd->pab', amplitudes, rounded, preferred_element_type=j...  22.7 us
  transfers between devices with their start and end apart: 3, of which 3 were waited for; matrix products, arithmetic and copies ran while one was open for 2% of the time, Pallas kernels for 0%

commit v1 on v0

--- a/solution.py
+++ b/solution.py
@@ -2,6 +2,18 @@
 import jax.numpy as jnp
 from jax import lax
 from jax.sharding import PartitionSpec as P
+
+
+def doubled_up(array, axis, dim):
+    ways, here, step = (lax.axis_size(axis), lax.axis_index(axis), array.shape[dim])
+    line, have = (array, 1)
+    while have < ways:
+        line = jnp.concatenate(
+            [line, lax.ppermute(line, axis, [(d, (d - have) % ways) for d in range(ways)])],
+            axis=dim,
+        )
+        have = 2 * have
+    return jnp.roll(line, here * step, axis=dim)
 
 
 def contract_aux(left_rows, right_rows):
@@ -16,7 +28,7 @@
     width_b = right_factor.shape[0]
     span_d = right_factor.shape[1]
     pair_count = amplitudes.shape[2]
-    left_all = lax.all_gather(left_factor, "col", axis=0, tiled=True)
+    left_all = doubled_up(left_factor, "col", 0)
     left_flat = left_all.reshape(left_all.shape[0], width_a * span_c)
     shard_part = lax.all_gather(right_factor, "row", axis=2, tiled=True)
     length = shard_part.shape[2]

time: 754 us -> 605 us (0.80)
  waiting for transfers between devices: 565 us -> 393 us
  other arithmetic: 0 us -> 9.02 us
    ppermute x0 -> x2, waiting for transfers between devices: none -> 336 us  [doubled_up(): lax.ppermute(line, axis, [(d, (d - have) % ways) for d in range(ways)])]
    all_gather x1, waiting for transfers between devices: 286 us -> 0.01 us  [on_device(): shard_part = lax.all_gather(right_factor, 'row', axis=2, tiled=True)]
    all_gather x1 -> x0, waiting for transfers between devices: 222 us -> none  [on_device(): left_all = lax.all_gather(left_factor, 'col', axis=0, tiled=True)]
    concatenate x0 -> x1, other arithmetic: none -> 9.02 us  [doubled_up(): jnp.concatenate([line, lax.ppermute(line, axis, [(d, (d - have) % ways) f...]
    unnamed x2 -> x13, local copies, waits for them, and re-layouts: 36.5 us -> 39 us
  transfers between devices with their start and end apart: 3 -> 4, of which waited for: 3 -> 3; matrix products, arithmetic and copies ran while one was open for 2% -> 5% of each run, Pallas kernels for 0% -> 0%
where the time goes in v1:
time: 605 us; the launch traced here: 604 us
  waiting for transfers between devices  393 us (65%)
  matrix products  138 us (23%)
  local copies, waits for them, and re-layouts  44.6 us (7%)
  between operations  13.5 us (2%)
  other arithmetic  9.02 us (1%)
  starting transfers between devices  6.53 us (1%)
    ppermute x2, waiting for transfers between devices, doubled_up(): lax.ppermute(line, axis, [(d, (d - have) % ways) for d in range(ways)])  336 us
    dot_general x1, matrix products, contract_aux(): lax.dot_general(left_rows, right_rows, (((0,), (1,)), ((), ())), preferre...  115 us
    reduce_scatter x1, waiting for transfers between devices, on_device(): lax.psum_scatter(partial_sums, ('row', 'col'), scatter_dimension=0, tiled...  55.9 us
    unnamed x13, local copies, waits for them, and re-layouts  39 us
    dot_general x1, matrix products, on_device(): jnp.einsum('cdp,acbd->pab', amplitudes, rounded, preferred_element_type=j...  22.7 us
  transfers between devices with their start and end apart: 4, of which 3 were waited for; matrix products, arithmetic and copies ran while one was open for 5% of the time, Pallas kernels for 0%

profile of v1, /device:TPU:0, one launch (start us, length us, event | category | flops | bytes accessed | tf_op | source)
XLA Modules:
  0.0 604.4 jit_solution(13533256620622418636)
XLA Ops:
  6.5 0.0 copy-start
  6.5 0.0 all-gather.2.cloned.1.call-start
  6.5 0.7 all-gather.2.cloned.1.call-update
  7.3 0.0 reduce-scatter.2.cloned.1.call-start
  7.3 5.1 collective-permute-start
  12.4 67.7 %collective-permute-done = bf16[768,8,256]{2,1,0:T(8,128)(2,1)S(1)} collective-permute-done((bf16[768,8,256]{2,1,0:T(8,128)(2,1)}, bf16[768,8,256]{2,1,0:T(8,128)(2,1)S(1)}, u32[]{:S(2)}, u32[]{:S(2)}) %collective-permute-start) | collective-permute-done | bytes 3145760 | tf_op jit(solution)/shard_map/ppermute | solution.py:12
  80.1 0.0 copy-start.1
  80.1 1.6 copy-done.1
  81.7 9.0 %pad_maximum_fusion = bf16[1536,8,256]{2,1,0:T(8,128)(2,1)} fusion(bf16[768,8,256]{2,1,0:T(8,128)(2,1)S(1)} %collective-permute-done, bf16[768,8,256]{2,1,0:T(8,128)(2,1)} %param.3), kind=kLoop, calls=%fused_computation.4 | loop fusion | flops 3145728 | bytes 12582912 | tf_op jit(solution)/shard_map/concatenate | solution.py:11
  90.8 1.4 collective-permute-start.1
  92.1 0.0 copy-done
  92.1 0.0 copy-start.2
  92.1 0.2 constant_dynamic-update-slice_fusion.5
  92.3 2.2 constant_dynamic-update-slice_fusion.4
  94.6 268.6 %collective-permute-done.1 = bf16[1536,8,256]{2,1,0:T(8,128)(2,1)} collective-permute-done((bf16[1536,8,256]{2,1,0:T(8,128)(2,1)}, bf16[1536,8,256]{2,1,0:T(8,128)(2,1)}, u32[]{:S(2)}, u32[]{:S(2)}) %collective-permute-start.1) | collective-permute-done | bytes 6291488 | tf_op jit(solution)/shard_map/ppermute | solution.py:12
  363.2 3.8 constant_dynamic-update-slice_fusion.3
  367.0 0.2 constant_dynamic-update-slice_fusion.2
  367.3 0.0 copy-done.2
  367.3 0.2 constant_dynamic-update-slice_fusion.1
  367.5 3.8 constant_dynamic-update-slice_fusion
  371.3 0.9 constant_dynamic-slice_fusion
  372.2 7.6 %copy.6 = bf16[384,8,8,256]{3,1,2,0:T(8,128)(2,1)} copy(bf16[384,8,8,256]{3,2,1,0:T(8,128)(2,1)S(1)} %bitcast.22) | data formatting | bytes 25165824
  379.8 0.0 all-gather.2.cloned.1.call-done
  379.8 115.2 %convolution_convert_fusion = bf16[2048,8192]{1,0:T(8,128)(2,1)} fusion(bf16[3072,2048]{1,0:T(8,128)(2,1)} %bitcast.24, bf16[8192,3072]{1,0:T(8,128)(2,1)} %bitcast.26), kind=kOutput, calls=%fused_computation.3 | convolution fusion | flops 103095992320 | bytes 96468992 | tf_op jit(solution)/shard_map/dot_general | solution.py:20
  495.0 23.1 %copy.7 = bf16[256,8,32,256]{3,2,1,0:T(8,128)(2,1)} copy(bf16[256,8,32,256]{3,1,2,0:T(8,128)(2,1)} %bitcast.23) | data formatting | bytes 67108864
  518.1 22.7 %fusion = f32[8,32,256,1]{2,1,3,0:T(8,128)S(1)} fusion(bf16[256,256,256]{2,1,0:T(8,128)(2,1)} %param.5, bf16[8,256,32,256]{3,2,1,0:T(8,128)(2,1)} %bitcast.21), kind=kOutput, calls=%fused_computation | convolution fusion | flops 8589934592 | bytes 67371008 | tf_op jit(solution)/shard_map/cdp,acbd->pab/dot_general | solution.py:37
  540.8 0.8 copy.4
  541.6 0.0 reduce-scatter.2.cloned.1.call-update
  541.6 55.9 %reduce-scatter.2.cloned.1.call-done = f32[16,256]{1,0:T(8,128)} async-done(((f32[256,256]{1,0:T(8,128)}), f32[16,256]{1,0:T(8,128)}) %reduce-scatter.2.cloned.1.call-update) | async-done | bytes 16400 | tf_op jit(solution)/shard_map/reduce_scatter | solution.py:40
Async XLA Ops:
  6.5 85.6 %copy-start = (bf16[768,8,256]{2,1,0:T(8,128)(2,1)S(1)}, bf16[768,8,256]{2,1,0:T(8,128)(2,1)}, u32[]{:S(2)}) copy-start(bf16[768,8,256]{2,1,0:T(8,128)(2,1)} %param.3) | copy-start | bytes 9437188
  6.5 373.3 %all-gather.2.cloned.1.call-start = ((), (), s32[]{:S(2)}) async-start(), calls=%async_computation.1 | async-start | bytes 62914560 | tf_op jit(solution)/shard_map/all_gather | solution.py:33
  7.3 590.3 %reduce-scatter.2.cloned.1.call-start = ((), (), s32[]{:S(2)}) async-start(), calls=%async_computation.2 | async-start | bytes 278528 | tf_op jit(solution)/shard_map/reduce_scatter | solution.py:40
  7.3 72.8 %collective-permute-start = (bf16[768,8,256]{2,1,0:T(8,128)(2,1)}, bf16[768,8,256]{2,1,0:T(8,128)(2,1)S(1)}, u32[]{:S(2)}, u32[]{:S(2)}) collective-permute-start(bf16[768,8,256]{2,1,0:T(8,128)(2,1)} %param.3), channel_id=1, source_target_pairs={{0,3},{1,0},{2,1},{3,2},{4,7},{5,4},{6,5},{7,6},{8,11},{9,8},{10,9... | collective-permute-start | bytes 9437192 | tf_op jit(solution)/shard_map/ppermute | solution.py:12
  80.1 1.6 copy-start.1
  90.8 272.4 %collective-permute-start.1 = (bf16[1536,8,256]{2,1,0:T(8,128)(2,1)}, bf16[1536,8,256]{2,1,0:T(8,128)(2,1)}, u32[]{:S(2)}, u32[]{:S(2)}) collective-permute-start(bf16[1536,8,256]{2,1,0:T(8,128)(2,1)} %pad_maximum_fusion), channel_id=1, source_target_pairs={{0,2},{1,3},{2,0},{3,1},{4,6},{5,7},{6,4},{7,5},{8,10},{9,11},{10,... | collective-permute-start | bytes 18874376 | tf_op jit(solution)/shard_map/ppermute | solution.py:12
  92.1 275.1 %copy-start.2 = (bf16[768,8,256]{2,1,0:T(8,128)(2,1)S(1)}, bf16[768,8,256]{2,1,0:T(8,128)(2,1)}, u32[]{:S(2)}) copy-start(bf16[768,8,256]{2,1,0:T(8,128)(2,1)} %copy-done.1) | copy-start | bytes 9437188
Sparse Core Ops, SparseCore 0:
  8.9 302.2 all-gather.1
  541.7 55.7 reduce-scatter.1
